TPU v7x, 32 devices: a whole 2x2x4 slice. The times are simulated.
32 devices in a mesh: scen: 2 (over y), site: 4 (over z), sub: 2 (over x), var: 2 (over core).
Axes of the slice: x: 2, y: 2, z: 4, core: 2. Of those that a mesh axis runs over, the one named last changes fastest.
Arguments:
- green_tensor: bfloat16 [8, 2, 16, 2, 2, 3, 32, 6, 128], P(('scen', 'site'), 'sub', None, 'var'), parts along dimension 0, may hold values from -0.078125 to 0.078125
- rupture_spectra: bfloat16 [2, 2, 512, 6, 1024], P(None, None, ('scen', 'var'), None, ('sub', 'site')), parts along dimension 2, may hold values from -6 to 6
- pair_site: int32 [8, 2, 16], P(('scen', 'site'), 'sub'), parts along dimension 0, may hold values from 0 to 3, as said below
- pair_block: int32 [8, 2, 16], P(('scen', 'site'), 'sub'), parts along dimension 0, may hold values from 0 to 3, as said below
- pair_count: int32 [8, 2, 16], P(('scen', 'site'), 'sub'), parts along dimension 0, may hold values from 0 to 128, as said below
- band_offset: int32 [2], P('scen'), parts along dimension 0, may hold values from 0 to 127
Outputs:
- site_spectra: float32 [2, 2, 3, 256, 1024], P(None, None, None, 'var', ('scen', 'site', 'sub')), parts along dimension 4
There are 2 independent parts, one for each index of `scen`. A program takes and returns all parts, laid end to end along the dimension named above; each array names one. Nothing has to cross between parts.
Inputs may be any that keep to these rules, and one draw needn't show every extreme that they name: On each device the live slots come first and are followed by unused slots; live slots name distinct pairs; unused slots have pair_count 0. No device has more than 12 live slots, and some device of every draw has exactly 12. `pair_site`: site block within the device's 4 site blocks. `pair_block`: subfault block within the device's group of 4 blocks.
All inputs are finite; a program needn't handle non-finite values.
Results may differ from a plain program's by a relative error of at most 0.0003.
Values may be sent and summed in bfloat16 or wider, within the bound.
No kernel may reach another device: no remote copies, remote signals or barrier semaphores. Data moves between devices by JAX's collectives and lax.ppermute only.
A program may use at most 64 MiB of HBM per device.

v0:
```python
import jax
import jax.numpy as jnp
from jax import lax
from jax.sharding import PartitionSpec as P

FREQS = 2
SITE_BLOCKS = 4
CORNER = 48.0


def pair_terms(
    totals,
    tiles,
    spectra,
    spec_start,
    total_start,
    site_table,
    block_table,
    count_table,
    slot_count,
):
    width = tiles.shape[1]
    block_sites = tiles.shape[4]
    variants = spectra.shape[2]
    columns = jnp.arange(128, dtype=jnp.int32)

    def add_pair(slot, totals):
        tensor_tile = lax.dynamic_index_in_dim(tiles, slot, 0, keepdims=False)
        spectrum = lax.dynamic_slice(
            spectra, (spec_start, 0, 0, 0, block_table[slot] * 128), (width, 2, variants, 6, 128)
        )
        keep_mask = (columns < count_table[slot]).astype(spectrum.dtype)
        spectrum = spectrum * keep_mask
        products = jnp.einsum(
            "fpcsmk,fqvmk->fpqcvs", tensor_tile, spectrum, preferred_element_type=jnp.float32
        )
        real_part = products[:, 0, 0] - products[:, 1, 1]
        imag_part = products[:, 0, 1] + products[:, 1, 0]
        contrib = jnp.stack([real_part, imag_part], axis=1)
        corner = (total_start, 0, 0, 0, site_table[slot] * block_sites)
        current = lax.dynamic_slice(totals, corner, contrib.shape)
        return lax.dynamic_update_slice(totals, current + contrib, corner)

    return lax.fori_loop(0, slot_count, add_pair, totals)


def shards(green_tensor, rupture_spectra, pair_site, pair_block, pair_count, band_offset):
    site_table = pair_site[0, 0]
    block_table = pair_block[0, 0]
    count_table = pair_count[0, 0]
    block_sites = green_tensor.shape[6]
    site_width = SITE_BLOCKS * block_sites
    spectra = lax.all_gather(rupture_spectra, "site", axis=4, tiled=True)
    slot_count = green_tensor.shape[2]
    local_vars = spectra.shape[2]
    empty = jnp.zeros((FREQS, 2, 3, local_vars, site_width), jnp.float32)
    piece_start = jnp.int32(0)
    totals = pair_terms(
        empty,
        lax.all_gather(green_tensor, "var", axis=3, tiled=True)[0, 0],
        spectra,
        piece_start,
        piece_start,
        site_table,
        block_table,
        count_table,
        slot_count,
    )
    partial_value = lax.psum_scatter(totals, "sub", scatter_dimension=4, tiled=True)
    freq_index = (band_offset[0] + jnp.arange(FREQS, dtype=jnp.int32)).astype(jnp.float32)
    brune = 1.0 / (1.0 + (freq_index / CORNER) ** 2)
    return partial_value * brune[:, None, None, None, None]


def solution(mesh):
    return jax.shard_map(
        shards,
        mesh=mesh,
        in_specs=(
            P(("scen", "site"), "sub", None, "var", None, None, None, None, None),
            P(None, None, ("scen", "var"), None, ("sub", "site")),
            P(("scen", "site"), "sub", None),
            P(("scen", "site"), "sub", None),
            P(("scen", "site"), "sub", None),
            P("scen"),
        ),
        out_specs=P(None, None, None, "var", ("scen", "site", "sub")),
        check_vma=False,
    )
```

profile of v0, /device:TPU:0, one launch (start us, length us, event | category | flops | bytes accessed | tf_op | source)
XLA Modules:
  0.0 213.4 jit_solution(682382720835881932)
XLA Ops:
  6.5 0.7 all-gather.3.cloned.1.call-update
  7.3 0.7 all-gather.5.cloned.1.call-update
  8.1 67.0 %all-gather.3.cloned.1.call-done = bf16[2,2,128,6,512]{4,2,3,1,0:T(8,128)(2,1)} async-done(((bf16[2,2,128,6,128]{4,2,3,1,0:T(8,128)(2,1)}), bf16[2,2,128,6,512]{4,2,3,1,0:T(8,128)(2,1)}) %all-gather.3.cloned.1.call-update) | async-done | bytes 3145744 | tf_op jit(solution)/shard_map/all_gather | solution.py:53
  75.1 21.5 %all-gather.5.cloned.1.call-done = bf16[1,1,16,2,2,3,32,6,128]{8,6,7,5,4,3,2,1,0:T(8,128)(2,1)} async-done(((bf16[1,1,16,1,2,3,32,6,128]{8,6,7,5,4,3,2,1,0:T(8,128)(2,1)}), bf16[1,1,16,2,2,3,32,6,128]{8,6,7,5,4,3,2,1,0:T(8,128)(2,1)}) %all-gather.5.cloned.1.call-update) | async-done | bytes 9437200 | tf_op jit(solution)/shard_map/all_gather | solution.py:60
  96.7 88.6 %while.14 = (s32[]{:T(128)}, f32[2,2,3,128,128]{3,4,2,1,0:T(8,128)S(1)}, s32[16]{0:T(128)S(1)}, s32[16]{0:T(128)S(1)}, bf16[2,2,128,6,512]{4,2,3,1,0:T(8,128)(2,...) while((s32[]{:T(128)}, ...), condition=%wide.region_1.2_spmd.clone, body=%wide.region_0.1_spmd.clone.sunk | while | flops 152715536 | bytes 3343629 | solution.py:44
  98.0 0.6 dynamic_slice.69
  98.5 0.6 compare_convert_fusion.2
  99.2 1.7 convolution_bitcast_fusion.2
  101.0 0.6 dynamic_slice.67
  103.5 0.6 dynamic_slice.69
  104.1 0.6 compare_convert_fusion.2
  104.7 1.7 convolution_bitcast_fusion.2
  106.5 0.6 dynamic_slice.67
  109.0 0.6 dynamic_slice.69
  109.6 0.6 compare_convert_fusion.2
  110.2 1.7 convolution_bitcast_fusion.2
  114.6 0.6 dynamic_slice.69
  115.2 0.6 compare_convert_fusion.2
  115.8 1.7 convolution_bitcast_fusion.2
  117.6 0.6 dynamic_slice.67
  120.1 0.6 dynamic_slice.69
  120.7 0.6 compare_convert_fusion.2
  121.3 1.7 convolution_bitcast_fusion.2
  123.1 0.6 dynamic_slice.67
  125.7 0.6 dynamic_slice.69
  126.2 0.6 compare_convert_fusion.2
  126.9 1.7 convolution_bitcast_fusion.2
  128.7 0.6 dynamic_slice.67
  131.2 0.6 dynamic_slice.69
  131.8 0.6 compare_convert_fusion.2
  132.4 1.7 convolution_bitcast_fusion.2
  136.7 0.6 dynamic_slice.69
  137.3 0.6 compare_convert_fusion.2
  137.9 1.7 convolution_bitcast_fusion.2
  139.7 0.6 dynamic_slice.67
  142.3 0.6 dynamic_slice.69
  142.9 0.6 compare_convert_fusion.2
  143.5 1.7 convolution_bitcast_fusion.2
  145.3 0.6 dynamic_slice.67
  147.8 0.6 dynamic_slice.69
  148.4 0.6 compare_convert_fusion.2
  149.0 1.7 convolution_bitcast_fusion.2
  153.3 0.6 dynamic_slice.69
  153.9 0.6 compare_convert_fusion.2
  154.6 1.7 convolution_bitcast_fusion.2
  156.4 0.6 dynamic_slice.67
  158.9 0.6 dynamic_slice.69
  159.5 0.6 compare_convert_fusion.2
  160.1 1.7 convolution_bitcast_fusion.2
  164.4 0.6 dynamic_slice.69
  165.0 0.6 compare_convert_fusion.2
  165.6 1.7 convolution_bitcast_fusion.2
  167.4 0.6 dynamic_slice.67
  169.9 0.6 dynamic_slice.69
  170.5 0.6 compare_convert_fusion.2
  171.2 1.7 convolution_bitcast_fusion.2
  175.5 0.6 dynamic_slice.69
  176.1 0.6 compare_convert_fusion.2
  176.7 1.7 convolution_bitcast_fusion.2
  181.6 0.6 compare_convert_fusion.2
  182.2 1.7 convolution_bitcast_fusion.2
  185.4 0.9 copy-done
  186.9 18.1 %reduce-scatter.2.cloned.1.call-done = f32[2,2,3,128,64]{3,4,2,1,0:T(8,128)} async-done(((f32[2,2,3,128,128]{3,4,2,1,0:T(8,128)}), f32[2,2,3,128,64]{3,4,2,1,0:T(8,128)}) %reduce-scatter.2.cloned.1.call-update) | async-done | bytes 393232 | tf_op jit(solution)/shard_map/reduce_scatter | solution.py:69
  205.0 1.8 broadcast_multiply_fusion
  (101 shorter events, 15.8 us)
Async XLA Ops:
  6.5 90.2 %copy-start.1 = (s32[1,1,16]{2,1,0:T(1,128)S(1)}, s32[1,1,16]{2,1,0:T(1,128)}, u32[]{:S(2)}) copy-start(s32[1,1,16]{2,1,0:T(1,128)} %param.10) | copy-start | bytes 196
  6.5 90.2 %copy-start.2 = (s32[1,1,16]{2,1,0:T(1,128)S(1)}, s32[1,1,16]{2,1,0:T(1,128)}, u32[]{:S(2)}) copy-start(s32[1,1,16]{2,1,0:T(1,128)} %param.11) | copy-start | bytes 196
  6.5 90.2 %copy-start.3 = (s32[1,1,16]{2,1,0:T(1,128)S(1)}, s32[1,1,16]{2,1,0:T(1,128)}, u32[]{:S(2)}) copy-start(s32[1,1,16]{2,1,0:T(1,128)} %param.12) | copy-start | bytes 196
  6.5 68.5 %all-gather.3.cloned.1.call-start = ((), (), s32[]{:S(2)}) async-start(), calls=%async_computation.1 | async-start | bytes 3932160 | tf_op jit(solution)/shard_map/all_gather | solution.py:53
  7.3 89.4 %all-gather.5.cloned.1.call-start = ((), (), s32[]{:S(2)}) async-start(), calls=%async_computation.2 | async-start | bytes 14155776 | tf_op jit(solution)/shard_map/all_gather | solution.py:60
  8.0 197.0 %reduce-scatter.2.cloned.1.call-start = ((), (), s32[]{:S(2)}) async-start(), calls=%async_computation.3 | async-start | bytes 1179648 | tf_op jit(solution)/shard_map/reduce_scatter | solution.py:69
  185.3 0.9 copy-start
Sparse Core Ops, SparseCore 0:
  8.9 66.1 all-gather.2
  76.6 19.9 all-gather.4
  186.4 18.5 reduce-scatter.1
where the time goes:
time: 214 us; the launch traced here: 213 us
  waiting for transfers between devices  108 us (50%)
  local copies, waits for them, and re-layouts  29.8 us (14%)
  matrix products  27.9 us (13%)
  loops' own time  20.9 us (10%)
  between operations  13.8 us (6%)
  other arithmetic  12.8 us (6%)
    all_gather x1, waiting for transfers between devices, shards(): spectra = lax.all_gather(rupture_spectra, 'site', axis=4, tiled=True)  67 us
    dot_general x16, matrix products, add_pair(): jnp.einsum('fpcsmk,fqvmk->fpqcvs', tensor_tile, spectrum, preferred_eleme...  27.9 us
    all_gather x1, waiting for transfers between devices, shards(): lax.all_gather(green_tensor, 'var', axis=3, tiled=True)[0, 0]  21.5 us
    another operation x1, loops' own time, pair_terms(): return lax.fori_loop(0, slot_count, add_pair, totals)  20.9 us
    reduce_scatter x1, waiting for transfers between devices, shards(): lax.psum_scatter(totals, 'sub', scatter_dimension=4, tiled=True)  18.1 us
    convert_element_type x16, other arithmetic, add_pair(): keep_mask = (columns < count_table[slot]).astype(spectrum.dtype)  9.88 us
    dynamic_slice x16, local copies, waits for them, and re-layouts, add_pair(): keep_mask = (columns < count_table[slot]).astype(spectrum.dtype)  9.52 us
    dynamic_slice x16, local copies, waits for them, and re-layouts, add_pair(): corner = (total_start, 0, 0, 0, site_table[slot] * block_sites)  9.52 us
  transfers between devices with their start and end apart: 3, of which 3 were waited for; matrix products, arithmetic and copies ran while one was open for 0% of the time, Pallas kernels for 0%

commit v1 on v0

--- a/solution.py
+++ b/solution.py
@@ -50,7 +50,24 @@
     count_table = pair_count[0, 0]
     block_sites = green_tensor.shape[6]
     site_width = SITE_BLOCKS * block_sites
-    spectra = lax.all_gather(rupture_spectra, "site", axis=4, tiled=True)
+    ways, here, step = (lax.axis_size("site"), lax.axis_index("site"), rupture_spectra.shape[4])
+    dims = [n * ways if d == 4 else n for d, n in enumerate(rupture_spectra.shape)]
+    spectra = lax.dynamic_update_slice_in_dim(
+        jnp.zeros(dims, rupture_spectra.dtype), rupture_spectra, here * step, axis=4
+    )
+    going_up = going_down = rupture_spectra
+    for far in range(1, ways // 2 + 1):
+        going_up = lax.ppermute(going_up, "site", [(d, (d + 1) % ways) for d in range(ways)])
+        spectra = lax.dynamic_update_slice_in_dim(
+            spectra, going_up, (here - far) % ways * step, axis=4
+        )
+        if 2 * far < ways:
+            going_down = lax.ppermute(
+                going_down, "site", [(d, (d - 1) % ways) for d in range(ways)]
+            )
+            spectra = lax.dynamic_update_slice_in_dim(
+                spectra, going_down, (here + far) % ways * step, axis=4
+            )
     slot_count = green_tensor.shape[2]
     local_vars = spectra.shape[2]
     empty = jnp.zeros((FREQS, 2, 3, local_vars, site_width), jnp.float32)

time: 214 us -> 183 us (0.86)
  waiting for transfers between devices: 108 us -> 63.3 us
  local copies, waits for them, and re-layouts: 29.8 us -> 37.2 us
  starting transfers between devices: 0.08 us -> 5.09 us
    all_gather x1 -> x0, waiting for transfers between devices: 67 us -> none  [shards(): spectra = lax.all_gather(rupture_spectra, 'site', axis=4, tiled=True)]
    ppermute x0 -> x3, waiting for transfers between devices: none -> 46.3 us  [the longest x2 34.6 us: shards(): lax.ppermute(going_up, 'site', [(d, (d + 1) % ways) for d in range(ways)])]
    all_gather x1, waiting for transfers between devices: 21.5 us -> 0.01 us  [shards(): lax.all_gather(green_tensor, 'var', axis=3, tiled=True)[0, 0]]
    ppermute x0 -> x3, starting transfers between devices: none -> 5.05 us  [the longest x2 3.03 us: shards(): lax.ppermute(going_up, 'site', [(d, (d + 1) % ways) for d in range(ways)])]
    dynamic_update_slice x0 -> x4, local copies, waits for them, and re-layouts: none -> 4.04 us  [the longest x2 2.02 us: shards(): lax.dynamic_update_slice_in_dim(spectra, going_up, (here - far) % ways *...]
  transfers between devices with their start and end apart: 3 -> 5, of which waited for: 3 -> 4; matrix products, arithmetic and copies ran while one was open for 0% -> 3% of each run, Pallas kernels for 0% -> 0%
where the time goes in v1:
time: 183 us; the launch traced here: 182 us
  waiting for transfers between devices  63.3 us (35%)
  local copies, waits for them, and re-layouts  37.2 us (20%)
  matrix products  27.8 us (15%)
  loops' own time  21.5 us (12%)
  between operations  14.1 us (8%)
  other arithmetic  13.1 us (7%)
  starting transfers between devices  5.09 us (3%)
    ppermute x2, waiting for transfers between devices, shards(): lax.ppermute(going_up, 'site', [(d, (d + 1) % ways) for d in range(ways)])  34.6 us
    dot_general x16, matrix products, add_pair(): jnp.einsum('fpcsmk,fqvmk->fpqcvs', tensor_tile, spectrum, preferred_eleme...  27.8 us
    another operation x1, loops' own time, pair_terms(): return lax.fori_loop(0, slot_count, add_pair, totals)  21.5 us
    reduce_scatter x1, waiting for transfers between devices, shards(): lax.psum_scatter(totals, 'sub', scatter_dimension=4, tiled=True)  16.3 us
    ppermute x1, waiting for transfers between devices, shards(): lax.ppermute(going_down, 'site', [(d, (d - 1) % ways) for d in range(ways)])  11.7 us
    convert_element_type x16, other arithmetic, add_pair(): keep_mask = (columns < count_table[slot]).astype(spectrum.dtype)  10.2 us
    dynamic_slice x16, local copies, waits for them, and re-layouts, add_pair(): keep_mask = (columns < count_table[slot]).astype(spectrum.dtype)  9.84 us
    dynamic_slice x16, local copies, waits for them, and re-layouts, add_pair(): corner = (total_start, 0, 0, 0, site_table[slot] * block_sites)  9.84 us
  transfers between devices with their start and end apart: 5, of which 4 were waited for; matrix products, arithmetic and copies ran while one was open for 3% of the time, Pallas kernels for 0%

profile of v1, /device:TPU:0, one launch (start us, length us, event | category | flops | bytes accessed | tf_op | source)
XLA Modules:
  0.0 182.1 jit_solution(3191286904196241499)
XLA Ops:
  6.5 0.7 all-gather.2.cloned.1.call-update
  7.7 3.0 %collective-permute-start = (bf16[2,2,128,6,128]{4,2,3,1,0:T(8,128)(2,1)S(1)}, bf16[2,2,128,6,128]{4,2,3,1,0:T(8,128)(2,1)S(1)}, u32[]{:S(2)}, u32[]{:S(2)}) collective-permute-start(bf16[2,2,128,6,128]{4,2,3,1,0:T(8,128)(2,1)S(1)} %copy-done.1), channel_id=1, source_target_pairs={{0,4},{4,8},{8,12},{12,0},{1,5},{5,9},{9,13},{13,1},{2,6},{6,10},{... | collective-permute-start | bytes 2359304 | tf_op jit(solution)/shard_map/ppermute | solution.py:60
  10.7 2.0 %collective-permute-start.1 = (bf16[2,2,128,6,128]{4,2,3,1,0:T(8,128)(2,1)S(1)}, bf16[2,2,128,6,128]{4,2,3,1,0:T(8,128)(2,1)S(1)}, u32[]{:S(2)}, u32[]{:S(2)}) collective-permute-start(bf16[2,2,128,6,128]{4,2,3,1,0:T(8,128)(2,1)S(1)} %copy-done.1), channel_id=1, source_target_pairs={{0,12},{4,0},{8,4},{12,8},{1,13},{5,1},{9,5},{13,9},{2,14},{6,2},{... | collective-permute-start | bytes 2359304 | tf_op jit(solution)/shard_map/ppermute | solution.py:65
  12.7 18.4 %collective-permute-done = bf16[2,2,128,6,128]{4,2,3,1,0:T(8,128)(2,1)S(1)} collective-permute-done((bf16[2,2,128,6,128]{4,2,3,1,0:T(8,128)(2,1)S(1)}, bf16[2,2,128,6,128]{4,2,3,1,0:T(8,128)(2,1)S(1)}, u32[]{:S(2)}, u32[]{:S(2)}) %collective-permute-start) | collective-permute-done | bytes 786464 | tf_op jit(solution)/shard_map/ppermute | solution.py:60
  31.1 2.0 %broadcast_in_dim.11 = bf16[2,2,128,6,512]{4,2,3,1,0:T(8,128)(2,1)} broadcast(bf16[]{:T(256)} %constant.82.clone.1), dimensions={} | broadcast | bytes 3145730 | tf_op jit(solution)/shard_map/broadcast_in_dim | solution.py:56
  33.1 1.0 constant_dynamic-update-slice_fusion.3
  34.1 1.0 constant_dynamic-update-slice_fusion.2
  35.1 11.7 %collective-permute-done.1 = bf16[2,2,128,6,128]{4,2,3,1,0:T(8,128)(2,1)S(1)} collective-permute-done((bf16[2,2,128,6,128]{4,2,3,1,0:T(8,128)(2,1)S(1)}, bf16[2,2,128,6,128]{4,2,3,1,0:T(8,128)(2,1)S(1)}, u32[]{:S(2)}, u32[]{:S(2)}) %collective-permute-start.1) | collective-permute-done | bytes 786464 | tf_op jit(solution)/shard_map/ppermute | solution.py:65
  46.8 1.0 constant_dynamic-update-slice_fusion.1
  47.8 16.2 %collective-permute-done.2 = bf16[2,2,128,6,128]{4,2,3,1,0:T(8,128)(2,1)S(1)} collective-permute-done((bf16[2,2,128,6,128]{4,2,3,1,0:T(8,128)(2,1)S(1)}, bf16[2,2,128,6,128]{4,2,3,1,0:T(8,128)(2,1)S(1)}, u32[]{:S(2)}, u32[]{:S(2)}) %collective-permute-start.2) | collective-permute-done | bytes 786464 | tf_op jit(solution)/shard_map/ppermute | solution.py:60
  64.0 1.0 constant_dynamic-update-slice_fusion
  65.1 90.4 %while.14 = (s32[]{:T(128)}, f32[2,2,3,128,128]{3,4,2,1,0:T(8,128)S(1)}, s32[16]{0:T(128)S(1)}, s32[16]{0:T(128)S(1)}, bf16[2,2,128,6,512]{4,2,3,1,0:T(8,128)(2,...) while((s32[]{:T(128)}, ...), condition=%wide.region_1.2_spmd.clone, body=%wide.region_0.1_spmd.clone.sunk | while | flops 152715536 | bytes 3343629 | solution.py:44
  66.4 0.6 dynamic_slice.69
  67.0 0.6 compare_convert_fusion.2
  67.7 1.7 convolution_bitcast_fusion.2
  69.5 0.6 dynamic_slice.67
  72.1 0.6 dynamic_slice.69
  72.7 0.6 compare_convert_fusion.2
  73.3 1.7 convolution_bitcast_fusion.2
  75.1 0.6 dynamic_slice.67
  77.7 0.6 dynamic_slice.69
  78.3 0.6 compare_convert_fusion.2
  79.0 1.7 convolution_bitcast_fusion.2
  80.8 0.6 dynamic_slice.67
  83.4 0.6 dynamic_slice.69
  84.0 0.6 compare_convert_fusion.2
  84.6 1.7 convolution_bitcast_fusion.2
  86.4 0.6 dynamic_slice.67
  89.0 0.6 dynamic_slice.69
  89.6 0.6 compare_convert_fusion.2
  90.3 1.7 convolution_bitcast_fusion.2
  92.1 0.6 dynamic_slice.67
  94.7 0.6 dynamic_slice.69
  95.3 0.6 compare_convert_fusion.2
  95.9 1.7 convolution_bitcast_fusion.2
  97.7 0.6 dynamic_slice.67
  100.3 0.6 dynamic_slice.69
  100.9 0.6 compare_convert_fusion.2
  101.6 1.7 convolution_bitcast_fusion.2
  103.4 0.6 dynamic_slice.67
  106.0 0.6 dynamic_slice.69
  106.6 0.6 compare_convert_fusion.2
  107.2 1.7 convolution_bitcast_fusion.2
  109.0 0.6 dynamic_slice.67
  111.6 0.6 dynamic_slice.69
  112.2 0.6 compare_convert_fusion.2
  112.9 1.7 convolution_bitcast_fusion.2
  117.9 0.6 compare_convert_fusion.2
  118.5 1.7 convolution_bitcast_fusion.2
  123.5 0.6 compare_convert_fusion.2
  124.2 1.7 convolution_bitcast_fusion.2
  129.2 0.6 compare_convert_fusion.2
  129.8 1.7 convolution_bitcast_fusion.2
  134.8 0.6 compare_convert_fusion.2
  135.5 1.7 convolution_bitcast_fusion.2
  140.5 0.6 compare_convert_fusion.2
  141.1 1.7 convolution_bitcast_fusion.2
  146.1 0.6 compare_convert_fusion.2
  146.8 1.7 convolution_bitcast_fusion.2
  151.8 0.6 compare_convert_fusion.2
  152.4 1.7 convolution_bitcast_fusion.2
  155.6 0.9 copy-done
  157.1 16.3 %reduce-scatter.2.cloned.1.call-done = f32[2,2,3,128,64]{3,4,2,1,0:T(8,128)} async-done(((f32[2,2,3,128,128]{3,4,2,1,0:T(8,128)}), f32[2,2,3,128,64]{3,4,2,1,0:T(8,128)}) %reduce-scatter.2.cloned.1.call-update) | async-done | bytes 393232 | tf_op jit(solution)/shard_map/reduce_scatter | solution.py:86
  173.4 1.8 %broadcast_multiply_fusion = f32[2,2,3,128,64]{3,4,2,1,0:T(8,128)} fusion(f32[2,2,3,128,64]{3,4,2,1,0:T(8,128)} %reduce-scatter.2.cloned.1.call-done, f32[2]{0:T(128)S(1)} %add_divide_fusion), kind=kLoop, calls=%fused_computation.19 | loop fusion | flops 98304 | bytes 786440 | tf_op jit(solution)/shard_map/mul | solution.py:89
  (111 shorter events, 20.9 us)
Async XLA Ops:
  6.5 1.1 copy-start.1
  6.5 58.5 %all-gather.2.cloned.1.call-start = ((), (), s32[]{:S(2)}) async-start(), calls=%async_computation.1 | async-start | bytes 14155776 | tf_op jit(solution)/shard_map/all_gather | solution.py:77
  7.3 166.2 %reduce-scatter.2.cloned.1.call-start = ((), (), s32[]{:S(2)}) async-start(), calls=%async_computation.2 | async-start | bytes 1179648 | tf_op jit(solution)/shard_map/reduce_scatter | solution.py:86
  7.7 23.5 %collective-permute-start = (bf16[2,2,128,6,128]{4,2,3,1,0:T(8,128)(2,1)S(1)}, bf16[2,2,128,6,128]{4,2,3,1,0:T(8,128)(2,1)S(1)}, u32[]{:S(2)}, u32[]{:S(2)}) collective-permute-start(bf16[2,2,128,6,128]{4,2,3,1,0:T(8,128)(2,1)S(1)} %copy-done.1), channel_id=1, source_target_pairs={{0,4},{4,8},{8,12},{12,0},{1,5},{5,9},{9,13},{13,1},{2,6},{6,10},{... | collective-permute-start | bytes 2359304 | tf_op jit(solution)/shard_map/ppermute | solution.py:60
  10.7 36.1 %collective-permute-start.1 = (bf16[2,2,128,6,128]{4,2,3,1,0:T(8,128)(2,1)S(1)}, bf16[2,2,128,6,128]{4,2,3,1,0:T(8,128)(2,1)S(1)}, u32[]{:S(2)}, u32[]{:S(2)}) collective-permute-start(bf16[2,2,128,6,128]{4,2,3,1,0:T(8,128)(2,1)S(1)} %copy-done.1), channel_id=1, source_target_pairs={{0,12},{4,0},{8,4},{12,8},{1,13},{5,1},{9,5},{13,9},{2,14},{6,2},{... | collective-permute-start | bytes 2359304 | tf_op jit(solution)/shard_map/ppermute | solution.py:65
  31.1 32.9 %collective-permute-start.2 = (bf16[2,2,128,6,128]{4,2,3,1,0:T(8,128)(2,1)S(1)}, bf16[2,2,128,6,128]{4,2,3,1,0:T(8,128)(2,1)S(1)}, u32[]{:S(2)}, u32[]{:S(2)}) collective-permute-start(bf16[2,2,128,6,128]{4,2,3,1,0:T(8,128)(2,1)S(1)} %collective-permute-done), channel_id=1, source_target_pairs={{0,4},{4,8},{8,12},{12,0},{1,5},{5,9},{9,13},{13,1},{2,6},{6,10},{... | collective-permute-start | bytes 2359304 | tf_op jit(solution)/shard_map/ppermute | solution.py:60
  34.1 31.0 %copy-start.2 = (s32[1,1,16]{2,1,0:T(1,128)S(1)}, s32[1,1,16]{2,1,0:T(1,128)}, u32[]{:S(2)}) copy-start(s32[1,1,16]{2,1,0:T(1,128)} %param.10) | copy-start | bytes 196
  34.1 31.0 %copy-start.3 = (s32[1,1,16]{2,1,0:T(1,128)S(1)}, s32[1,1,16]{2,1,0:T(1,128)}, u32[]{:S(2)}) copy-start(s32[1,1,16]{2,1,0:T(1,128)} %param.11) | copy-start | bytes 196
  34.1 31.0 %copy-start.4 = (s32[1,1,16]{2,1,0:T(1,128)S(1)}, s32[1,1,16]{2,1,0:T(1,128)}, u32[]{:S(2)}) copy-start(s32[1,1,16]{2,1,0:T(1,128)} %param.12) | copy-start | bytes 196
  155.5 0.9 copy-start
Sparse Core Ops, SparseCore 0:
  8.9 24.4 all-gather.1
  156.6 16.7 reduce-scatter.1
